TPU v7x, 256 devices: a whole 4x4x8 slice. The times are simulated.
256 devices in a mesh: island: 8 (over y_lo, x), fsdp: 32 (over z, y_hi, core).
Axes of the slice: x: 4, y: 4 (y_hi: 2, y_lo: 2; y = y_hi * 2 + y_lo), z: 8, core: 2. Of those that a mesh axis runs over, the one named last changes fastest.
Arguments:
- global_params: bfloat16 [8, 1, 4096, 8192], P('island', None, 'fsdp'), may hold values from -6 to 6
- local_params: bfloat16 [8, 1, 4096, 8192], P('island', None, 'fsdp'), may hold values from -6 to 6
- momentum: bfloat16 [8, 1, 4096, 8192], P('island', None, 'fsdp'), may hold values from -6 to 6
- init_factors: float32 [4, 1, 4, 8192], replicated, may hold values from -6 to 6
- seeds: int32 [8], replicated, may hold values from 0 to 3, as said below
- plan: int32 [8], replicated, may hold values from 1 to 4, as said below
- round_index: int32 [], replicated, may hold values from 0 to 999
Outputs:
- new_params: bfloat16 [8, 1, 4096, 8192], P('island', None, 'fsdp')
- new_momentum: bfloat16 [8, 1, 4096, 8192], P('island', None, 'fsdp')
- warm_factors: float32 [8, 1, 4, 8192], P('island')
Inputs may be any that keep to these rules, and one draw needn't show every extreme that they name: `plan`: every entry is a power of two; every power of two up to 4 appears. `seeds`: every value from 0 to 3 is used by some replica.
All inputs are finite; a program needn't handle non-finite values.
Results may differ from a plain program's by a relative error of at most 0.0017.
Values sent between devices are 32-bit elements; how exact they have to be, the bound alone decides.
No kernel may reach another device: no remote copies, remote signals or barrier semaphores. Data moves between devices by JAX's collectives and lax.ppermute only.
A program may use at most 64 MiB of HBM per device.

v0:
```python
import jax
import jax.numpy as jnp
from jax import lax
from jax.sharding import PartitionSpec as P

ITERS = 3


def swapped(x, axis, apart):
    return lax.ppermute(x, axis, [(i, i ^ 1 << apart) for i in range(lax.axis_size(axis))])


def on_device(global_params, local_params, momentum, init_factors, seeds, plan, round_index):
    high = lax.Precision.HIGHEST
    offset = plan[jnp.mod(round_index, plan.shape[0])]
    island_pos = lax.axis_index("island")
    partner = jnp.bitwise_xor(island_pos, offset)
    factor = init_factors[seeds[jnp.minimum(island_pos, partner)]]
    start = global_params[0].astype(jnp.float32)
    delta = start - local_params[0].astype(jnp.float32)
    levels = lax.axis_size("island").bit_length() - 1
    level_ids = jnp.arange(levels, dtype=jnp.int32)
    which_bit = jnp.sum(jnp.where(jnp.left_shift(jnp.int32(1), level_ids) == offset, level_ids, 0))

    def make_branch(level):

        def one_level(values):
            return swapped(values, "island", level)

        return one_level

    def from_peer(values):
        branches = [make_branch(level) for level in range(levels)]
        return lax.switch(which_bit, branches, values)

    basis = None
    for turn in range(ITERS):
        mine_left = jnp.einsum("mkc,mrc->mkr", factor, delta, precision=high)
        left = mine_left - from_peer(mine_left)
        gram_part = jnp.einsum("mkr,mjr->mkj", left, left, precision=high)
        gram = lax.psum(gram_part, "fsdp")
        lower = jnp.linalg.cholesky(gram)
        basis = lax.linalg.triangular_solve(lower, left, left_side=True, lower=True)
        right_part = jnp.einsum("mkr,mrc->mkc", basis, delta, precision=high)
        mine_right = lax.psum(right_part, "fsdp")
        factor = mine_right + from_peer(mine_right)
    correction = jnp.einsum("mkr,mkc->mrc", basis, factor, precision=high)
    gossiped = delta - 0.5 * correction
    velocity = 0.9 * momentum[0].astype(jnp.float32) + gossiped
    updated = start - 0.7 * (gossiped + 0.9 * velocity)
    return (updated.astype(jnp.bfloat16)[None], velocity.astype(jnp.bfloat16)[None], factor[None])


def solution(mesh):
    return jax.shard_map(
        on_device,
        mesh=mesh,
        in_specs=(
            P("island", None, "fsdp", None),
            P("island", None, "fsdp", None),
            P("island", None, "fsdp", None),
            P(),
            P(),
            P(),
            P(),
        ),
        out_specs=(
            P("island", None, "fsdp", None),
            P("island", None, "fsdp", None),
            P("island", None, None, None),
        ),
        check_vma=False,
    )
```

profile of v0, /device:TPU:2, one launch (start us, length us, event | category | flops | bytes accessed | tf_op | source)
XLA Modules:
  0.0 1050.5 jit_solution(16679805387560155915)
XLA Ops:
  15.0 5.2 fusion.17
  20.1 5.2 conditional.6
  26.3 71.8 %psum.69 = f32[1,4,4]{1,2,0:T(4,128)S(1)} all-reduce(f32[1,4,4]{1,2,0:T(4,128)S(1)} %convolution_bitcast_fusion.5), channel_id=1, replica_groups=mesh['island'=8,'fsdp'=32] {'fsdp'}, use_global_device_ids=true, to_apply=%region_4.5 | all-reduce | flops 16 | bytes 128 | tf_op jit(solution)/shard_map/psum | solution.py:41
  101.1 4.7 convolution_bitcast_fusion.2
  105.8 243.2 %all-reduce.4.cloned.1.call-done = f32[1,4,8192]{2,1,0:T(4,128)} async-done(((f32[1,4,8192]{2,1,0:T(4,128)}), f32[1,4,8192]{2,1,0:T(4,128)}) %all-reduce.4.cloned.1.call-update) | async-done | bytes 131088 | tf_op jit(solution)/shard_map/psum | solution.py:45
  349.0 6.8 conditional.7
  351.1 4.7 collective-permute-done.4
  355.8 5.1 fusion.20
  360.9 5.2 conditional.8
  362.9 3.1 collective-permute-done.7
  366.9 65.5 %psum.71 = f32[1,4,4]{1,2,0:T(4,128)S(1)} all-reduce(f32[1,4,4]{1,2,0:T(4,128)S(1)} %convolution_bitcast_fusion.4), channel_id=1, replica_groups=mesh['island'=8,'fsdp'=32] {'fsdp'}, use_global_device_ids=true, to_apply=%region_14.17 | all-reduce | flops 16 | bytes 128 | tf_op jit(solution)/shard_map/psum | solution.py:41
  435.5 4.7 convolution_bitcast_fusion.1
  440.2 247.2 %all-reduce.6.cloned.1.call-done = f32[1,4,8192]{2,1,0:T(4,128)} async-done(((f32[1,4,8192]{2,1,0:T(4,128)}), f32[1,4,8192]{2,1,0:T(4,128)}) %all-reduce.6.cloned.1.call-update) | async-done | bytes 131088 | tf_op jit(solution)/shard_map/psum | solution.py:45
  687.4 6.8 conditional.9
  689.5 4.7 collective-permute-done.10
  694.2 5.1 fusion.23
  699.3 5.2 conditional.10
  701.4 3.1 collective-permute-done.13
  705.4 65.5 %psum.73 = f32[1,4,4]{1,2,0:T(4,128)S(1)} all-reduce(f32[1,4,4]{1,2,0:T(4,128)S(1)} %convolution_bitcast_fusion.3), channel_id=1, replica_groups=mesh['island'=8,'fsdp'=32] {'fsdp'}, use_global_device_ids=true, to_apply=%region_22.25 | all-reduce | flops 16 | bytes 128 | tf_op jit(solution)/shard_map/psum | solution.py:41
  773.9 4.7 convolution_bitcast_fusion
  778.6 247.3 %all-reduce.8.cloned.1.call-done = f32[1,4,8192]{2,1,0:T(4,128)} async-done(((f32[1,4,8192]{2,1,0:T(4,128)}), f32[1,4,8192]{2,1,0:T(4,128)}) %all-reduce.8.cloned.1.call-update) | async-done | bytes 131088 | tf_op jit(solution)/shard_map/psum | solution.py:45
  1025.9 6.8 conditional.11
  1028.0 4.7 collective-permute-done.16
  1034.4 9.6 fusion.15
  (48 shorter events, 32.9 us)
Async XLA Ops:
  7.2 7.8 copy-start
  7.2 341.8 %all-reduce.4.cloned.1.call-start = ((), (), s32[]{:S(2)}) async-start(), calls=%async_computation | async-start | bytes 262144 | tf_op jit(solution)/shard_map/psum | solution.py:45
  15.0 86.1 %copy-start.1 = (bf16[1,1,128,8192]{3,2,1,0:T(8,128)(2,1)S(1)}, bf16[1,1,128,8192]{3,2,1,0:T(8,128)(2,1)}, u32[]{:S(2)}) copy-start(bf16[1,1,128,8192]{3,2,1,0:T(8,128)(2,1)} %param.28) | copy-start | bytes 6291460
  20.1 5.2 collective-permute-start.1
  105.8 581.7 %all-reduce.6.cloned.1.call-start = ((), (), s32[]{:S(2)}) async-start(), calls=%async_computation.1 | async-start | bytes 262144 | tf_op jit(solution)/shard_map/psum | solution.py:45
  349.0 6.8 collective-permute-start.4
  360.9 5.2 collective-permute-start.7
  440.2 585.7 %all-reduce.8.cloned.1.call-start = ((), (), s32[]{:S(2)}) async-start(), calls=%async_computation.2 | async-start | bytes 262144 | tf_op jit(solution)/shard_map/psum | solution.py:45
  687.4 6.8 collective-permute-start.10
  699.3 5.2 collective-permute-start.13
  1025.9 6.8 collective-permute-start.16
Sparse Core Ops, SparseCore 0:
  105.9 243.0 all-reduce.3
  440.3 247.1 all-reduce.5
  778.8 247.1 all-reduce.7
where the time goes:
time: 1050 us
  waiting for transfers between devices  761 us (72%)
  blocking collectives  203 us (19%)
  matrix products  44.2 us (4%)
  between operations  17.8 us (2%)
  starting transfers between devices  12.7 us (1%)
    psum x3, waiting for transfers between devices, on_device(): mine_right = lax.psum(right_part, 'fsdp')  738 us
    psum x3, blocking collectives, on_device(): gram = lax.psum(gram_part, 'fsdp')  203 us
    ppermute x6, waiting for transfers between devices, swapped(): lax.ppermute(x, axis, [(i, i ^ 1 << apart) for i in range(lax.axis_size(a...  23.4 us
  transfers between devices with their start and end apart: 9, of which 9 were waited for; matrix products, arithmetic and copies ran while one was open for 0% of the time, Pallas kernels for 0%

commit v1 on v0

--- a/solution.py
+++ b/solution.py
@@ -38,7 +38,7 @@
         mine_left = jnp.einsum("mkc,mrc->mkr", factor, delta, precision=high)
         left = mine_left - from_peer(mine_left)
         gram_part = jnp.einsum("mkr,mjr->mkj", left, left, precision=high)
-        gram = lax.psum(gram_part, "fsdp")
+        gram = jnp.sum(lax.all_gather(gram_part, "fsdp"), axis=0)
         lower = jnp.linalg.cholesky(gram)
         basis = lax.linalg.triangular_solve(lower, left, left_side=True, lower=True)
         right_part = jnp.einsum("mkr,mrc->mkc", basis, delta, precision=high)

time: 1050 us -> 971 us (0.925)
  blocking collectives: 203 us -> 119 us
    psum x3 -> x0, blocking collectives: 203 us -> none  [on_device(): gram = lax.psum(gram_part, 'fsdp')]
    all_gather x0 -> x3, blocking collectives: none -> 119 us  [on_device(): gram = jnp.sum(lax.all_gather(gram_part, 'fsdp'), axis=0)]
where the time goes in v1:
time: 971 us
  waiting for transfers between devices  765 us (79%)
  blocking collectives  119 us (12%)
  matrix products  44.2 us (5%)
  between operations  17.8 us (2%)
  starting transfers between devices  12.8 us (1%)
    psum x3, waiting for transfers between devices, on_device(): mine_right = lax.psum(right_part, 'fsdp')  742 us
    all_gather x3, blocking collectives, on_device(): gram = jnp.sum(lax.all_gather(gram_part, 'fsdp'), axis=0)  119 us
    ppermute x6, waiting for transfers between devices, swapped(): lax.ppermute(x, axis, [(i, i ^ 1 << apart) for i in range(lax.axis_size(a...  23.4 us
  transfers between devices with their start and end apart: 9, of which 9 were waited for; matrix products, arithmetic and copies ran while one was open for 0% of the time, Pallas kernels for 0%

profile of v1, /device:TPU:2, one launch (start us, length us, event | category | flops | bytes accessed | tf_op | source)
XLA Modules:
  0.0 970.7 jit_solution(10544233522459926555)
XLA Ops:
  15.0 5.2 fusion.17
  20.1 5.2 conditional.6
  26.3 45.0 %all-gather.3 = f32[32,4,4]{2,1,0:T(4,128)S(1)} all-gather(f32[1,4,4]{2,1,0:T(4,128)S(1)} %convolution_bitcast_fusion.5), channel_id=2, replica_groups=mesh['island'=8,'fsdp'=32] {'fsdp'}, dimensions={0}, use_global_device_ids=true | all-gather | bytes 2112 | tf_op jit(solution)/shard_map/all_gather | solution.py:41
  74.3 4.7 convolution_bitcast_fusion.2
  79.1 244.4 %all-reduce.4.cloned.1.call-done = f32[1,4,8192]{2,1,0:T(4,128)} async-done(((f32[1,4,8192]{2,1,0:T(4,128)}), f32[1,4,8192]{2,1,0:T(4,128)}) %all-reduce.4.cloned.1.call-update) | async-done | bytes 131088 | tf_op jit(solution)/shard_map/psum | solution.py:45
  323.5 6.8 conditional.7
  325.6 4.7 collective-permute-done.4
  330.3 5.1 fusion.20
  335.4 5.4 conditional.8
  337.7 3.1 collective-permute-done.7
  341.7 36.8 %all-gather.4 = f32[32,4,4]{2,1,0:T(4,128)S(1)} all-gather(f32[1,4,4]{2,1,0:T(4,128)S(1)} %convolution_bitcast_fusion.4), channel_id=3, replica_groups=mesh['island'=8,'fsdp'=32] {'fsdp'}, dimensions={0}, use_global_device_ids=true | all-gather | bytes 2112 | tf_op jit(solution)/shard_map/all_gather | solution.py:41
  381.5 4.7 convolution_bitcast_fusion.1
  386.3 248.7 %all-reduce.6.cloned.1.call-done = f32[1,4,8192]{2,1,0:T(4,128)} async-done(((f32[1,4,8192]{2,1,0:T(4,128)}), f32[1,4,8192]{2,1,0:T(4,128)}) %all-reduce.6.cloned.1.call-update) | async-done | bytes 131088 | tf_op jit(solution)/shard_map/psum | solution.py:45
  635.0 6.8 conditional.9
  637.1 4.7 collective-permute-done.10
  641.8 5.1 fusion.23
  646.9 5.2 conditional.10
  649.0 3.1 collective-permute-done.13
  653.0 37.0 %all-gather.5 = f32[32,4,4]{2,1,0:T(4,128)S(1)} all-gather(f32[1,4,4]{2,1,0:T(4,128)S(1)} %convolution_bitcast_fusion.3), channel_id=4, replica_groups=mesh['island'=8,'fsdp'=32] {'fsdp'}, dimensions={0}, use_global_device_ids=true | all-gather | bytes 2112 | tf_op jit(solution)/shard_map/all_gather | solution.py:41
  693.1 4.7 convolution_bitcast_fusion
  697.8 248.4 %all-reduce.8.cloned.1.call-done = f32[1,4,8192]{2,1,0:T(4,128)} async-done(((f32[1,4,8192]{2,1,0:T(4,128)}), f32[1,4,8192]{2,1,0:T(4,128)}) %all-reduce.8.cloned.1.call-update) | async-done | bytes 131088 | tf_op jit(solution)/shard_map/psum | solution.py:45
  946.1 6.8 conditional.11
  948.2 4.7 collective-permute-done.16
  954.6 9.6 fusion.15
  (51 shorter events, 33.1 us)
Async XLA Ops:
  7.2 7.8 copy-start
  7.2 316.3 %all-reduce.4.cloned.1.call-start = ((), (), s32[]{:S(2)}) async-start(), calls=%async_computation | async-start | bytes 262144 | tf_op jit(solution)/shard_map/psum | solution.py:45
  15.0 59.4 %copy-start.1 = (bf16[1,1,128,8192]{3,2,1,0:T(8,128)(2,1)S(1)}, bf16[1,1,128,8192]{3,2,1,0:T(8,128)(2,1)}, u32[]{:S(2)}) copy-start(bf16[1,1,128,8192]{3,2,1,0:T(8,128)(2,1)} %param.28) | copy-start | bytes 6291460
  20.1 5.2 collective-permute-start.1
  79.0 556.0 %all-reduce.6.cloned.1.call-start = ((), (), s32[]{:S(2)}) async-start(), calls=%async_computation.1 | async-start | bytes 262144 | tf_op jit(solution)/shard_map/psum | solution.py:45
  323.5 6.8 collective-permute-start.4
  335.5 5.3 collective-permute-start.7
  386.2 559.9 %all-reduce.8.cloned.1.call-start = ((), (), s32[]{:S(2)}) async-start(), calls=%async_computation.2 | async-start | bytes 262144 | tf_op jit(solution)/shard_map/psum | solution.py:45
  635.0 6.8 collective-permute-start.10
  646.9 5.2 collective-permute-start.13
  946.1 6.8 collective-permute-start.16
Sparse Core Ops, SparseCore 0:
  79.1 244.3 all-reduce.3
  386.3 248.6 all-reduce.5
  697.9 248.1 all-reduce.7
